TPU v7x, 32 devices: a whole 2x2x4 slice. The times are simulated.
32 devices in a mesh: dp: 8 (over z, x), tensor: 4 (over y, core).
Axes of the slice: x: 2, y: 2, z: 4, core: 2. Of those that a mesh axis runs over, the one named last changes fastest.
Arguments:
- tokens: bfloat16 [3072, 1024], P('dp'), may hold values from -6 to 6
- segment_ids: int32 [8, 384], P('dp'), may hold values from 0 to 5, never falling along the last dimension, each value on 1 to 192 neighbouring positions
- cotangent: bfloat16 [3072, 1024], P('dp'), may hold values from -6 to 6
- norm1_gain: float32 [1024], replicated, may hold values from 0.5 to 1.5
- norm1_shift: float32 [1024], replicated, may hold values from -3 to 3
- w_qkv: bfloat16 [1024, 3072], P(None, 'tensor'), may hold values from -0.1875 to 0.1875
- b_qkv: float32 [3072], P('tensor'), may hold values from -9 to 9
- w_dense: bfloat16 [1024, 1024], P('tensor'), may hold values from -0.75 to 0.75
- b_dense: float32 [1024], replicated, may hold values from -3 to 3
- norm2_gain: float32 [1024], replicated, may hold values from 0.5 to 1.5
- norm2_shift: float32 [1024], replicated, may hold values from -3 to 3
- w_up: bfloat16 [1024, 4096], P(None, 'tensor'), may hold values from -0.1875 to 0.1875
- b_up: float32 [4096], P('tensor'), may hold values from -3 to 3
- w_down: bfloat16 [4096, 1024], P('tensor'), may hold values from -0.09375 to 0.09375
- b_down: float32 [1024], replicated, may hold values from -3 to 3
Outputs:
- output: bfloat16 [3072, 1024], P('dp')
- grad_input: float32 [3072, 1024], P('dp')
- grad_norm1_gain: float32 [1024], P('dp')
- grad_norm1_shift: float32 [1024], P('dp')
- grad_w_qkv: float32 [1024, 3072], P('dp', 'tensor')
- grad_b_qkv: float32 [3072], P(('tensor', 'dp'))
- grad_w_dense: float32 [1024, 1024], P('tensor', 'dp')
- grad_b_dense: float32 [1024], P('dp')
- grad_norm2_gain: float32 [1024], P('dp')
- grad_norm2_shift: float32 [1024], P('dp')
- grad_w_up: float32 [1024, 4096], P('dp', 'tensor')
- grad_b_up: float32 [4096], P(('tensor', 'dp'))
- grad_w_down: float32 [4096, 1024], P('tensor', 'dp')
- grad_b_down: float32 [1024], P('dp')
Inputs may be any that keep to these rules, and one draw needn't show every extreme that they name: `segment_ids`: in each row, ids never fall; each of the 6 sequences has 1 to 192 tokens and one has exactly 192.
All inputs are finite; a program needn't handle non-finite values.
Results may differ from a plain program's by a relative error of at most 0.019.
The roundings to bfloat16 on the way count: a program that leaves them out, or rounds other values in their place, can miss the bound.
Values sent between devices are 32-bit elements; how exact they have to be, the bound alone decides.
A program may use at most 128 MiB of HBM per device.

v0:
```python
import math

import jax
import jax.numpy as jnp
from jax import lax
from jax.sharding import PartitionSpec as P

H = 16
HD = 64


EPSILON = 1e-05
GELU_COEF = math.sqrt(2.0 / math.pi)


def layer_norm(values, gain, shift):
    average = jnp.mean(values, axis=-1, keepdims=True)
    centered = values - average
    variance = jnp.mean(centered * centered, axis=-1, keepdims=True)
    inverse = lax.rsqrt(variance + EPSILON)
    normed = centered * inverse
    return (normed * gain + shift, normed, inverse)


def norm_backward(upstream, normed, inverse, gain):
    scaled = upstream * gain
    return inverse * (
        scaled
        - jnp.mean(scaled, axis=-1, keepdims=True)
        - normed * jnp.mean(scaled * normed, axis=-1, keepdims=True)
    )


def gelu_pair(inputs):
    tangent = jnp.tanh(GELU_COEF * (inputs + 0.044715 * inputs * inputs * inputs))
    result = 0.5 * inputs * (1.0 + tangent)
    derivative = 0.5 * (1.0 + tangent) + 0.5 * inputs * (1.0 - tangent * tangent) * GELU_COEF * (
        1.0 + 3.0 * 0.044715 * inputs * inputs
    )
    return (result, derivative)


def head_scores(queries, key_vecs, slopes, offset, allowed, scaling):
    raw_scores = jnp.einsum("ihe,jhe->hij", queries, key_vecs, preferred_element_type=jnp.float32)
    return jnp.where(
        allowed[None], raw_scores * scaling + slopes[:, None, None] * offset[None], -1e30
    )


def local(
    tokens,
    segment_ids,
    cotangent,
    norm1_gain,
    norm1_shift,
    w_qkv,
    b_qkv,
    w_dense,
    b_dense,
    norm2_gain,
    norm2_shift,
    w_up,
    b_up,
    w_down,
    b_down,
):
    segments = segment_ids[0]
    row_count = tokens.shape[0]
    heads_here = w_qkv.shape[1] // (3 * HD)
    head_start = lax.axis_index("tensor") * heads_here
    scaling = 1.0 / math.sqrt(HD)
    slopes = 2.0 ** (-8.0 * (head_start + jnp.arange(heads_here) + 1).astype(jnp.float32) / H)
    places = jnp.arange(row_count)
    offset = (places[None, :] - places[:, None]).astype(jnp.float32)
    allowed = (segments[:, None] == segments[None, :]) & (places[None, :] <= places[:, None])
    inputs = tokens.astype(jnp.float32)
    first_out, normed1, inverse1 = layer_norm(inputs, norm1_gain, norm1_shift)
    first_in = first_out.astype(jnp.bfloat16)
    joined = (jnp.dot(first_in, w_qkv, preferred_element_type=jnp.float32) + b_qkv).astype(
        jnp.bfloat16
    )
    joined = joined.reshape(row_count, heads_here, 3, HD)
    queries = joined[:, :, 0]
    key_vecs = joined[:, :, 1]
    val_vecs = joined[:, :, 2]
    scores = head_scores(queries, key_vecs, slopes, offset, allowed, scaling)
    highest = jnp.max(scores, axis=-1, keepdims=True)
    log_total = highest + jnp.log(jnp.sum(jnp.exp(scores - highest), axis=-1, keepdims=True))
    probs_b = jnp.exp(scores - log_total).astype(jnp.bfloat16)
    context = jnp.einsum(
        "hij,jhe->ihe", probs_b, val_vecs, preferred_element_type=jnp.float32
    ).astype(jnp.bfloat16)
    context = context.reshape(row_count, heads_here * HD)
    attended = lax.psum(jnp.dot(context, w_dense, preferred_element_type=jnp.float32), "tensor")
    hidden = inputs + attended + b_dense
    second_out, normed2, inverse2 = layer_norm(hidden, norm2_gain, norm2_shift)
    second_in = second_out.astype(jnp.bfloat16)
    upward = jnp.dot(second_in, w_up, preferred_element_type=jnp.float32) + b_up
    activated, gelu_slope = gelu_pair(upward)
    activated_b = activated.astype(jnp.bfloat16)
    mixed = lax.psum(jnp.dot(activated_b, w_down, preferred_element_type=jnp.float32), "tensor")
    output = (hidden + mixed + b_down).astype(jnp.bfloat16)
    grad_out = cotangent.astype(jnp.float32)
    grad_w_down = jnp.dot(activated_b.T, cotangent, preferred_element_type=jnp.float32)
    grad_b_down = jnp.sum(grad_out, axis=0)
    grad_up = jnp.dot(cotangent, w_down.T, preferred_element_type=jnp.float32) * gelu_slope
    grad_up_b = grad_up.astype(jnp.bfloat16)
    grad_w_up = jnp.dot(second_in.T, grad_up_b, preferred_element_type=jnp.float32)
    grad_b_up = jnp.sum(grad_up, axis=0)
    grad_norm2 = lax.psum(jnp.dot(grad_up_b, w_up.T, preferred_element_type=jnp.float32), "tensor")
    grad_gain2 = jnp.sum(grad_norm2 * normed2, axis=0)
    grad_shift2 = jnp.sum(grad_norm2, axis=0)
    grad_hidden = grad_out + norm_backward(grad_norm2, normed2, inverse2, norm2_gain)
    grad_hidden_b = grad_hidden.astype(jnp.bfloat16)
    grad_w_dense = jnp.dot(context.T, grad_hidden_b, preferred_element_type=jnp.float32)
    grad_b_dense = jnp.sum(grad_hidden, axis=0)
    grad_context = jnp.dot(grad_hidden_b, w_dense.T, preferred_element_type=jnp.float32).astype(
        jnp.bfloat16
    )
    grad_context = grad_context.reshape(row_count, heads_here, HD)
    scores_again = head_scores(queries, key_vecs, slopes, offset, allowed, scaling)
    probs_again = jnp.exp(scores_again - log_total)
    probs_again_b = probs_again.astype(jnp.bfloat16)
    grad_vals = jnp.einsum(
        "hij,ihe->jhe", probs_again_b, grad_context, preferred_element_type=jnp.float32
    )
    grad_probs = jnp.einsum(
        "ihe,jhe->hij", grad_context, val_vecs, preferred_element_type=jnp.float32
    )
    row_inner = jnp.sum(probs_again * grad_probs, axis=-1, keepdims=True)
    grad_scores = (probs_again * (grad_probs - row_inner)).astype(jnp.bfloat16)
    grad_queries = (
        jnp.einsum("hij,jhe->ihe", grad_scores, key_vecs, preferred_element_type=jnp.float32)
        * scaling
    )
    grad_keys = (
        jnp.einsum("hij,ihe->jhe", grad_scores, queries, preferred_element_type=jnp.float32)
        * scaling
    )
    grad_joined = jnp.stack([grad_queries, grad_keys, grad_vals], axis=2).reshape(
        row_count, 3 * heads_here * HD
    )
    grad_joined_b = grad_joined.astype(jnp.bfloat16)
    grad_w_qkv = jnp.dot(first_in.T, grad_joined_b, preferred_element_type=jnp.float32)
    grad_b_qkv = jnp.sum(grad_joined, axis=0)
    grad_norm1 = lax.psum(
        jnp.dot(grad_joined_b, w_qkv.T, preferred_element_type=jnp.float32), "tensor"
    )
    grad_gain1 = jnp.sum(grad_norm1 * normed1, axis=0)
    grad_shift1 = jnp.sum(grad_norm1, axis=0)
    grad_input = grad_hidden + norm_backward(grad_norm1, normed1, inverse1, norm1_gain)
    summed = (
        lax.psum_scatter(grad_gain1, "dp", scatter_dimension=0, tiled=True),
        lax.psum_scatter(grad_shift1, "dp", scatter_dimension=0, tiled=True),
        lax.psum_scatter(grad_w_qkv, "dp", scatter_dimension=0, tiled=True),
        lax.psum_scatter(grad_b_qkv, "dp", scatter_dimension=0, tiled=True),
        lax.psum_scatter(grad_w_dense, "dp", scatter_dimension=1, tiled=True),
        lax.psum_scatter(grad_b_dense, "dp", scatter_dimension=0, tiled=True),
        lax.psum_scatter(grad_gain2, "dp", scatter_dimension=0, tiled=True),
        lax.psum_scatter(grad_shift2, "dp", scatter_dimension=0, tiled=True),
        lax.psum_scatter(grad_w_up, "dp", scatter_dimension=0, tiled=True),
        lax.psum_scatter(grad_b_up, "dp", scatter_dimension=0, tiled=True),
        lax.psum_scatter(grad_w_down, "dp", scatter_dimension=1, tiled=True),
        lax.psum_scatter(grad_b_down, "dp", scatter_dimension=0, tiled=True),
    )
    return (output, grad_input) + tuple(summed)


def solution(mesh):
    in_specs = (
        P("dp", None),
        P("dp", None),
        P("dp", None),
        P(),
        P(),
        P(None, "tensor"),
        P("tensor"),
        P("tensor", None),
        P(),
        P(),
        P(),
        P(None, "tensor"),
        P("tensor"),
        P("tensor", None),
        P(),
    )
    out_specs = (
        P("dp", None),
        P("dp", None),
        P("dp"),
        P("dp"),
        P("dp", "tensor"),
        P(("tensor", "dp")),
        P("tensor", "dp"),
        P("dp"),
        P("dp"),
        P("dp"),
        P("dp", "tensor"),
        P(("tensor", "dp")),
        P("tensor", "dp"),
        P("dp"),
    )
    return jax.shard_map(local, mesh=mesh, in_specs=in_specs, out_specs=out_specs, check_vma=False)
```

profile of v0, /device:TPU:0, one launch (start us, length us, event | category | flops | bytes accessed | tf_op | source)
XLA Modules:
  0.0 535.8 jit_solution(16800177713516023344)
XLA Ops:
  9.9 3.1 fusion.22
  15.2 1.9 fusion.46
  20.8 45.7 %all-reduce.14.cloned.1.call-done = f32[384,1024]{1,0:T(8,128)} async-done(((f32[384,1024]{1,0:T(8,128)}), f32[384,1024]{1,0:T(8,128)}) %all-reduce.14.cloned.1.call-update) | async-done | bytes 1572880 | tf_op jit(solution)/shard_map/psum | solution.py:94
  66.5 1.8 fusion.44
  70.7 1.8 fusion.47
  73.4 2.2 fusion.33
  75.8 3.7 fusion.42
  79.5 39.1 %all-reduce.16.cloned.1.call-done = f32[384,1024]{1,0:T(8,128)} async-done(((f32[384,1024]{1,0:T(8,128)}), f32[384,1024]{1,0:T(8,128)}) %all-reduce.16.cloned.1.call-update) | async-done | bytes 1572880 | tf_op jit(solution)/shard_map/psum | solution.py:110
  118.6 2.7 multiply_reduce_fusion.1
  121.5 2.0 fusion.43
  128.2 2.0 fusion.49
  130.2 2.9 fusion.28
  133.2 3.0 fusion.38
  136.3 5.0 fusion.31
  141.3 5.0 fusion.41
  150.3 48.5 %all-reduce.18.cloned.1.call-done = (f32[384,1024]{1,0:T(8,128)}, f32[384,1024]{1,0:T(8,128)}) async-done(((f32[384,1024]{1,0:T(8,128)}, f32[384,1024]{1,0:T(8,128)}), (f32[384,1024]{1,0:T(8,128)}, f32[384,1024]{1,0:T(8,128)})) %all-reduce.18.cloned.1.call-update) | async-done | bytes 3145744 | tf_op jit(solution)/shard_map/psum | solution.py:101
  198.9 2.1 fusion.13
  201.0 37.3 %all-reduce.8 = (f32[1024]{0:T(1024)S(1)}, f32[1024]{0:T(1024)S(1)}, f32[768]{0:T(1024)S(1)}, f32[1024]{0:T(1024)S(1)}, f32[1024]{0:T(1024)S(1)}, /*index=5*/f32...) all-reduce(f32[1024]{0:T(1024)S(1)} %get-tuple-element.16, ...), channel_id=2, replica_groups=mesh['dp'=8,'tensor'=4] {'dp'}, use_global_device_ids=true, to_apply=%region_16.17.clone | all-reduce | flops 7936 | bytes 63488
  243.0 3.3 add_convert_fusion
  246.2 1.7 fusion.12
  247.9 19.6 %reduce-scatter.7.cloned.1.call-done = f32[256,128]{1,0:T(8,128)} async-done(((f32[256,1024]{1,0:T(8,128)}), f32[256,128]{1,0:T(8,128)}) %reduce-scatter.7.cloned.1.call-update) | async-done | bytes 131088 | tf_op jit(solution)/shard_map/reduce_scatter | solution.py:157
  267.5 77.4 %reduce-scatter.5.cloned.1.call-done = f32[128,768]{1,0:T(8,128)} async-done(((f32[1024,768]{1,0:T(8,128)}), f32[128,768]{1,0:T(8,128)}) %reduce-scatter.5.cloned.1.call-update) | async-done | bytes 393232 | tf_op jit(solution)/shard_map/reduce_scatter | solution.py:155
  345.0 91.5 %reduce-scatter.9.cloned.1.call-done = f32[128,1024]{1,0:T(8,128)} async-done(((f32[1024,1024]{1,0:T(8,128)}), f32[128,1024]{1,0:T(8,128)}) %reduce-scatter.9.cloned.1.call-update) | async-done | bytes 524304 | tf_op jit(solution)/shard_map/reduce_scatter | solution.py:161
  436.5 92.5 %reduce-scatter.11.cloned.1.call-done = f32[1024,128]{1,0:T(8,128)} async-done(((f32[1024,1024]{1,0:T(8,128)}), f32[1024,128]{1,0:T(8,128)}) %reduce-scatter.11.cloned.1.call-update) | async-done | bytes 524304 | tf_op jit(solution)/shard_map/reduce_scatter | solution.py:163
  (118 shorter events, 24.0 us)
Async XLA Ops:
  7.2 63.5 %copy-start = (bf16[1024,1024]{1,0:T(8,128)(2,1)S(1)}, bf16[1024,1024]{1,0:T(8,128)(2,1)}, u32[]{:S(2)}) copy-start(bf16[1024,1024]{1,0:T(8,128)(2,1)} %param.28) | copy-start | bytes 6291460
  7.2 2.3 copy-start.5
  7.2 2.6 copy-start.23
  7.2 2.6 copy-start.24
  7.2 2.6 copy-start.29
  7.2 59.3 %all-reduce.14.cloned.1.call-start = ((), (), s32[]{:S(2)}) async-start(), calls=%async_computation.4 | async-start | bytes 3145728 | tf_op jit(solution)/shard_map/psum | solution.py:94
  9.9 4.5 copy-start.27
  19.2 47.3 %copy-start.26 = (f32[1024]{0:T(1024)S(1)}, f32[1024]{0:T(1024)}, u32[]{:S(2)}) copy-start(f32[1024]{0:T(1024)} %param.23) | copy-start | bytes 12292
  20.8 97.9 %all-reduce.16.cloned.1.call-start = ((), (), s32[]{:S(2)}) async-start(), calls=%async_computation.5 | async-start | bytes 3145728 | tf_op jit(solution)/shard_map/psum | solution.py:110
  66.5 3.0 copy-start.28
  70.7 1.8 copy-start.15
  75.6 123.3 %all-reduce.18.cloned.1.call-start = ((), (), s32[]{:S(2)}) async-start(), calls=%async_computation.10 | async-start | bytes 6291456 | tf_op jit(solution)/shard_map/psum | solution.py:101
  118.6 2.7 copy-start.2
  118.6 2.8 copy-start.9
  121.5 2.1 copy-start.17
  121.5 2.5 copy-start.4
  130.2 137.4 %reduce-scatter.7.cloned.1.call-start = ((), (), s32[]{:S(2)}) async-start(), calls=%async_computation.7 | async-start | bytes 1179648 | tf_op jit(solution)/shard_map/reduce_scatter | solution.py:157
  133.2 211.8 %reduce-scatter.5.cloned.1.call-start = ((), (), s32[]{:S(2)}) async-start(), calls=%async_computation.6 | async-start | bytes 3538944 | tf_op jit(solution)/shard_map/reduce_scatter | solution.py:155
  136.2 300.2 %reduce-scatter.9.cloned.1.call-start = ((), (), s32[]{:S(2)}) async-start(), calls=%async_computation.8 | async-start | bytes 4718592 | tf_op jit(solution)/shard_map/reduce_scatter | solution.py:161
  141.3 387.7 %reduce-scatter.11.cloned.1.call-start = ((), (), s32[]{:S(2)}) async-start(), calls=%async_computation.9 | async-start | bytes 4718592 | tf_op jit(solution)/shard_map/reduce_scatter | solution.py:163
  146.3 2.5 copy-start.11
  148.9 94.1 %copy-start.25 = (f32[1024]{0:T(1024)S(1)}, f32[1024]{0:T(1024)}, u32[]{:S(2)}) copy-start(f32[1024]{0:T(1024)} %param.29) | copy-start | bytes 12292
  242.9 3.3 copy-start.7
  243.0 3.3 copy-start.8
  (15 other events, 16.4 us)
Sparse Core Ops, SparseCore 0:
  20.9 45.5 all-reduce.13
  75.7 42.9 all-reduce.15
  130.3 68.5 all-reduce.17
  202.7 64.7 reduce-scatter.6
  271.5 73.3 reduce-scatter.4
  349.0 87.3 reduce-scatter.8
  440.7 88.2 reduce-scatter.10
where the time goes:
time: 536 us
  waiting for transfers between devices  415 us (77%)
  blocking collectives  37.3 us (7%)
  matrix products  36.2 us (7%)
  other arithmetic  19.6 us (4%)
  between operations  15.8 us (3%)
  local copies, waits for them, and re-layouts  11.9 us (2%)
    reduce_scatter x1, waiting for transfers between devices, local(): lax.psum_scatter(grad_w_down, 'dp', scatter_dimension=1, tiled=True)  92.5 us
    reduce_scatter x1, waiting for transfers between devices, local(): lax.psum_scatter(grad_w_up, 'dp', scatter_dimension=0, tiled=True)  91.5 us
    reduce_scatter x1, waiting for transfers between devices, local(): lax.psum_scatter(grad_w_qkv, 'dp', scatter_dimension=0, tiled=True)  77.4 us
    psum x1, waiting for transfers between devices, local(): lax.psum(jnp.dot(activated_b, w_down, preferred_element_type=jnp.float32)...  48.5 us
    psum x1, waiting for transfers between devices, local(): lax.psum(jnp.dot(context, w_dense, preferred_element_type=jnp.float32), '...  45.7 us
    psum x1, waiting for transfers between devices, local(): lax.psum(jnp.dot(grad_up_b, w_up.T, preferred_element_type=jnp.float32),...  39.1 us
    unnamed x1, blocking collectives  37.3 us
    reduce_scatter x1, waiting for transfers between devices, local(): lax.psum_scatter(grad_w_dense, 'dp', scatter_dimension=1, tiled=True)  19.6 us
  transfers between devices with their start and end apart: 7, of which 7 were waited for; matrix products, arithmetic and copies ran while one was open for 6% of the time, Pallas kernels for 0%

commit v1 on v0

--- a/solution.py
+++ b/solution.py
@@ -1,8 +1,11 @@
+import functools
 import math
 
 import jax
 import jax.numpy as jnp
 from jax import lax
+from jax.experimental import pallas as pl
+from jax.experimental.pallas import tpu as pltpu
 from jax.sharding import PartitionSpec as P
 
 H = 16
@@ -46,8 +49,285 @@
         allowed[None], raw_scores * scaling + slopes[:, None, None] * offset[None], -1e30
     )
 
+CHUNKS = 4
+LAG = 2
+MESH = pl.DeviceIdType.MESH
+MIB = 1024 * 1024
+
+
+def add_rows(dst, terms):
+    rows, columns = dst.shape
+    step = math.gcd(rows, 32 if columns > 128 else 256)
+
+    def body(i, carry):
+        part = pl.ds(pl.multiple_of(i * step, step), step)
+        total = terms[0][part, :]
+        for term in terms[1:]:
+            total = total + term[part, :]
+        dst[part, :] = total
+        return carry
+
+    lax.fori_loop(0, rows // step, body, 0)
+
+
+def exchange_kernel(kinds, n_sum, *refs):
+    n_red = len(kinds)
+    refs = list(refs)
+
+    def take(count):
+        taken = refs[:count]
+        del refs[:count]
+        return taken
+
+    grads, parts = take(n_red), take(n_sum)
+    outs, sums = take(n_red), take(n_sum)
+    rx, ru, rd = take(n_red), take(n_red), take(n_red)
+    if n_red:
+        xs, xr, us, ur, ds, dr = take(6)
+    if n_sum:
+        near, mine, far = take(3)
+        cs, cr, ys, yr, bs, br = take(6)
+    barrier = pltpu.get_barrier_semaphore()
+    expected = 0
+    if n_red:
+        place = lax.axis_index("dp")
+        z, x = place // 2, place % 2
+        other_x = {"dp": z * 2 + 1 - x}
+        above, below = {"dp": place + 2}, {"dp": place - 2}
+        pl.semaphore_signal(barrier, inc=1, device_id=other_x, device_id_type=MESH)
+        low, high = z > 0, z < 3
+
+        @pl.when(high)
+        def _():
+            pl.semaphore_signal(barrier, inc=1, device_id=above, device_id_type=MESH)
+
+        @pl.when(low)
+        def _():
+            pl.semaphore_signal(barrier, inc=1, device_id=below, device_id_type=MESH)
+
+        expected = expected + 1 + jnp.minimum(z, 1) + jnp.minimum(3 - z, 1)
+    if n_sum:
+        seat = lax.axis_index("tensor")
+        y, core = seat // 2, seat % 2
+        other_core = {"tensor": y * 2 + 1 - core}
+        other_y = {"tensor": (1 - y) * 2 + core}
+        pl.semaphore_signal(barrier, inc=1, device_id=other_core, device_id_type=MESH)
+        pl.semaphore_signal(barrier, inc=1, device_id=other_y, device_id_type=MESH)
+        expected = expected + 2
+    pl.semaphore_wait(barrier, expected)
+
+    def shard(m, target, column):
+        ref = grads[m]
+        index = 2 * target + column
+        if kinds[m] == "rows":
+            size = ref.shape[0] // 8
+            return ref.at[pl.ds(pl.multiple_of(index * size, size), size), :]
+        size = ref.shape[1] // 8
+        return ref.at[:, pl.ds(pl.multiple_of(index * size, size), size)]
+
+    def send(src, dst, send_sem, recv_sem, device):
+        return pltpu.make_async_remote_copy(
+            src_ref=src,
+            dst_ref=dst,
+            send_sem=send_sem,
+            recv_sem=recv_sem,
+            device_id=device,
+            device_id_type=MESH,
+        )
+
+    def across(m, t):
+        return send(shard(m, t, 1 - x), rx[m].at[t], xs.at[m, t], xr.at[m, t], other_x)
+
+    def up(m, t):
+        return send(rx[m].at[t], ru[m].at[t], us.at[m, t], ur.at[m, t], above)
+
+    def down(m, t):
+        return send(rx[m].at[t], rd[m].at[t], ds.at[m, t], dr.at[m, t], below)
+
+    def near_copy(a, k):
+        half = parts[a].shape[0] // 2
+        size = half // CHUNKS
+        start = pl.multiple_of((1 - core) * half + k * size, 8)
+        return send(
+            parts[a].at[pl.ds(start, size), :],
+            near.at[a, k],
+            cs.at[a, k],
+            cr.at[a, k],
+            other_core,
+        )
+
+    def far_copy(a, k):
+        return send(mine.at[a, k], far.at[a, k], ys.at[a, k], yr.at[a, k], other_y)
+
+    def own(a, k):
+        half = parts[a].shape[0] // 2
+        size = half // CHUNKS
+        return pl.ds(pl.multiple_of(core * half + k * size, 8), size)
+
+    def back_copy(a, k):
+        rows = own(a, k)
+        return send(
+            sums[a].at[rows, :], sums[a].at[rows, :], bs.at[a, k], br.at[a, k], other_core
+        )
+
+    for a in range(n_sum):
+        for k in range(CHUNKS):
+            near_copy(a, k).start()
+    order = [(m, t) for m in range(n_red) for t in (3, 0, 2, 1)]
+    for m, t in order:
+        across(m, t).start()
+
+    def open_sum(a, k):
+        near_copy(a, k).wait_recv()
+        add_rows(mine.at[a, k], [parts[a].at[own(a, k), :], near.at[a, k]])
+        far_copy(a, k).start()
+
+    def close_sum(a, k):
+        far_copy(a, k).wait_recv()
+        add_rows(sums[a].at[own(a, k), :], [mine.at[a, k], far.at[a, k]])
+        back_copy(a, k).start()
+
+    def first_hop(m, t):
+        across(m, t).wait_recv()
+        add_rows(rx[m].at[t], [shard(m, t, x), rx[m].at[t]])
+        if t > 0:
+
+            @pl.when(z == 0)
+            def _():
+                up(m, t).start()
+
+        if t < 3:
+
+            @pl.when(z == 3)
+            def _():
+                down(m, t).start()
+
+    def next_hop(m, t):
+        @pl.when((z > 0) & (z < t))
+        def _():
+            up(m, t).wait_recv()
+            add_rows(rx[m].at[t], [rx[m].at[t], ru[m].at[t]])
+            up(m, t).start()
+
+        @pl.when((z < 3) & (z > t))
+        def _():
+            down(m, t).wait_recv()
+            add_rows(rx[m].at[t], [rx[m].at[t], rd[m].at[t]])
+            down(m, t).start()
+
+    def last_hop(m, t):
+        @pl.when(z == t)
+        def _():
+            terms = [rx[m].at[t]]
+            if t > 0:
+                up(m, t).wait_recv()
+                terms.append(ru[m].at[t])
+            if t < 3:
+                down(m, t).wait_recv()
+                terms.append(rd[m].at[t])
+            add_rows(outs[m], terms)
+
+    for a in range(n_sum):
+        for k in range(CHUNKS):
+            open_sum(a, k)
+    closing = [(a, k) for a in range(n_sum) for k in range(CHUNKS)]
+    for n in range(len(order) + LAG):
+        if n > 0 or not order:
+            for _ in range(CHUNKS):
+                if closing:
+                    close_sum(*closing.pop(0))
+        if n < len(order):
+            first_hop(*order[n])
+        if n >= LAG and order:
+            next_hop(*order[n - LAG])
+    while closing:
+        close_sum(*closing.pop(0))
+    for m, t in order:
+        last_hop(m, t)
+    for a in range(n_sum):
+        for k in range(CHUNKS):
+            back_copy(a, k).wait_recv()
+            near_copy(a, k).wait_send()
+            far_copy(a, k).wait_send()
+            back_copy(a, k).wait_send()
+    for m, t in order:
+        across(m, t).wait_send()
+
+        @pl.when(z < t)
+        def _():
+            up(m, t).wait_send()
+
+        @pl.when(z > t)
+        def _():
+            down(m, t).wait_send()
+
+
+def exchange(grads, kinds, parts, collective_id):
+    n_red, n_sum = len(grads), len(parts)
+    f32 = jnp.float32
+    shapes = []
+    for grad, kind in zip(grads, kinds):
+        rows, columns = grad.shape
+        shapes.append((rows // 8, columns) if kind == "rows" else (rows, columns // 8))
+    out_shape = [jax.ShapeDtypeStruct(s, f32) for s in shapes]
+    out_shape += [jax.ShapeDtypeStruct(p.shape, f32) for p in parts]
+    scratch = []
+    if n_red:
+        for _ in range(3):
+            scratch += [pltpu.VMEM((4,) + s, f32) for s in shapes]
+        scratch += [pltpu.SemaphoreType.DMA((n_red, 4))] * 6
+    if n_sum:
+        rows, columns = parts[0].shape
+        scratch += [pltpu.VMEM((n_sum, CHUNKS, rows // 2 // CHUNKS, columns), f32)] * 3
+        scratch += [pltpu.SemaphoreType.DMA((n_sum, CHUNKS))] * 6
+    vmem = pl.BlockSpec(memory_space=pltpu.VMEM)
+    return pl.pallas_call(
+        functools.partial(exchange_kernel, tuple(kinds), n_sum),
+        out_shape=out_shape,
+        in_specs=[vmem] * (n_red + n_sum),
+        out_specs=[vmem] * (n_red + n_sum),
+        scratch_shapes=scratch,
+        compiler_params=pltpu.CompilerParams(
+            collective_id=collective_id, has_side_effects=True, vmem_limit_bytes=56 * MIB
+        ),
+    )(*grads, *parts)
+
+
+def paired(size_tensor):
+    return size_tensor == 4
+
+
+def sum_parts(parts, size_tensor, collective_id):
+    if paired(size_tensor):
+        return exchange([], [], parts, collective_id)
+    return [lax.psum(part, "tensor") for part in parts]
+
+
+def scatter(grads, kinds, parts, sizes, collective_id):
+    if sizes == (8, 4):
+        done = exchange(grads, kinds, parts, collective_id)
+        return done[: len(grads)], done[len(grads) :]
+    reduced = [
+        lax.psum_scatter(g, "dp", scatter_dimension=0 if k == "rows" else 1, tiled=True)
+        for g, k in zip(grads, kinds)
+    ]
+    return reduced, (sum_parts(parts, sizes[1], collective_id) if parts else [])
+
+
+def scatter_vectors(vectors, sizes, collective_id):
+    n_dp = sizes[0]
+    widths = [v.shape[0] // n_dp for v in vectors]
+    widest = -(-max(widths) // 128) * 128
+    table = jnp.stack(
+        [jnp.pad(v.reshape(n_dp, -1), ((0, 0), (0, widest - w))) for v, w in zip(vectors, widths)],
+        axis=1,
+    ).reshape(n_dp * len(vectors), widest)
+    (mine,), _ = scatter([table], ["rows"], [], sizes, collective_id)
+    return [mine[i, :w] for i, w in enumerate(widths)]
+
 
 def local(
+    sizes,
     tokens,
     segment_ids,
     cotangent,
@@ -91,15 +371,16 @@
         "hij,jhe->ihe", probs_b, val_vecs, preferred_element_type=jnp.float32
     ).astype(jnp.bfloat16)
     context = context.reshape(row_count, heads_here * HD)
-    attended = lax.psum(jnp.dot(context, w_dense, preferred_element_type=jnp.float32), "tensor")
+    (attended,) = sum_parts(
+        [jnp.dot(context, w_dense, preferred_element_type=jnp.float32)], sizes[1], 0
+    )
     hidden = inputs + attended + b_dense
     second_out, normed2, inverse2 = layer_norm(hidden, norm2_gain, norm2_shift)
     second_in = second_out.astype(jnp.bfloat16)
     upward = jnp.dot(second_in, w_up, preferred_element_type=jnp.float32) + b_up
     activated, gelu_slope = gelu_pair(upward)
     activated_b = activated.astype(jnp.bfloat16)
-    mixed = lax.psum(jnp.dot(activated_b, w_down, preferred_element_type=jnp.float32), "tensor")
-    output = (hidden + mixed + b_down).astype(jnp.bfloat16)
+    mixed = jnp.dot(activated_b, w_down, preferred_element_type=jnp.float32)
     grad_out = cotangent.astype(jnp.float32)
     grad_w_down = jnp.dot(activated_b.T, cotangent, preferred_element_type=jnp.float32)
     grad_b_down = jnp.sum(grad_out, axis=0)
@@ -107,7 +388,11 @@
     grad_up_b = grad_up.astype(jnp.bfloat16)
     grad_w_up = jnp.dot(second_in.T, grad_up_b, preferred_element_type=jnp.float32)
     grad_b_up = jnp.sum(grad_up, axis=0)
-    grad_norm2 = lax.psum(jnp.dot(grad_up_b, w_up.T, preferred_element_type=jnp.float32), "tensor")
+    grad_norm2 = jnp.dot(grad_up_b, w_up.T, preferred_element_type=jnp.float32)
+    (grad_w_up, grad_w_down), (grad_norm2, mixed) = scatter(
+        [grad_w_up, grad_w_down], ["rows", "columns"], [grad_norm2, mixed], sizes, 1
+    )
+    output = (hidden + mixed + b_down).astype(jnp.bfloat16)
     grad_gain2 = jnp.sum(grad_norm2 * normed2, axis=0)
     grad_shift2 = jnp.sum(grad_norm2, axis=0)
     grad_hidden = grad_out + norm_backward(grad_norm2, normed2, inverse2, norm2_gain)
@@ -143,27 +428,44 @@
     grad_joined_b = grad_joined.astype(jnp.bfloat16)
     grad_w_qkv = jnp.dot(first_in.T, grad_joined_b, preferred_element_type=jnp.float32)
     grad_b_qkv = jnp.sum(grad_joined, axis=0)
-    grad_norm1 = lax.psum(
-        jnp.dot(grad_joined_b, w_qkv.T, preferred_element_type=jnp.float32), "tensor"
+    grad_norm1 = jnp.dot(grad_joined_b, w_qkv.T, preferred_element_type=jnp.float32)
+    (grad_w_qkv, grad_w_dense), (grad_norm1,) = scatter(
+        [grad_w_qkv, grad_w_dense], ["rows", "columns"], [grad_norm1], sizes, 2
     )
     grad_gain1 = jnp.sum(grad_norm1 * normed1, axis=0)
     grad_shift1 = jnp.sum(grad_norm1, axis=0)
     grad_input = grad_hidden + norm_backward(grad_norm1, normed1, inverse1, norm1_gain)
-    summed = (
-        lax.psum_scatter(grad_gain1, "dp", scatter_dimension=0, tiled=True),
-        lax.psum_scatter(grad_shift1, "dp", scatter_dimension=0, tiled=True),
-        lax.psum_scatter(grad_w_qkv, "dp", scatter_dimension=0, tiled=True),
-        lax.psum_scatter(grad_b_qkv, "dp", scatter_dimension=0, tiled=True),
-        lax.psum_scatter(grad_w_dense, "dp", scatter_dimension=1, tiled=True),
-        lax.psum_scatter(grad_b_dense, "dp", scatter_dimension=0, tiled=True),
-        lax.psum_scatter(grad_gain2, "dp", scatter_dimension=0, tiled=True),
-        lax.psum_scatter(grad_shift2, "dp", scatter_dimension=0, tiled=True),
-        lax.psum_scatter(grad_w_up, "dp", scatter_dimension=0, tiled=True),
-        lax.psum_scatter(grad_b_up, "dp", scatter_dimension=0, tiled=True),
-        lax.psum_scatter(grad_w_down, "dp", scatter_dimension=1, tiled=True),
-        lax.psum_scatter(grad_b_down, "dp", scatter_dimension=0, tiled=True),
-    )
-    return (output, grad_input) + tuple(summed)
+    vectors = scatter_vectors(
+        [
+            grad_gain1,
+            grad_shift1,
+            grad_b_qkv,
+            grad_b_dense,
+            grad_gain2,
+            grad_shift2,
+            grad_b_up,
+            grad_b_down,
+        ],
+        sizes,
+        3,
+    )
+    gain1, shift1, b_qkv_part, b_dense_part, gain2, shift2, b_up_part, b_down_part = vectors
+    return (
+        output,
+        grad_input,
+        gain1,
+        shift1,
+        grad_w_qkv,
+        b_qkv_part,
+        grad_w_dense,
+        b_dense_part,
+        gain2,
+        shift2,
+        grad_w_up,
+        b_up_part,
+        grad_w_down,
+        b_down_part,
+    )
 
 
 def solution(mesh):
@@ -200,4 +502,6 @@
         P("tensor", "dp"),
         P("dp"),
     )
-    return jax.shard_map(local, mesh=mesh, in_specs=in_specs, out_specs=out_specs, check_vma=False)
+    sizes = (mesh.shape["dp"], mesh.shape["tensor"])
+    body = functools.partial(local, sizes)
+    return jax.shard_map(body, mesh=mesh, in_specs=in_specs, out_specs=out_specs, check_vma=False)

time: 536 us -> 298 us (0.56)
  waiting for transfers between devices: 415 us -> 0 us
  Pallas kernels: 0 us -> 239 us
  blocking collectives: 37.3 us -> 0 us
  between operations: 15.8 us -> 1.07 us
    reduce_scatter x4 -> x0, waiting for transfers between devices: 281 us -> none  [the longest x1 92.5 us: local(): lax.psum_scatter(grad_w_down, 'dp', scatter_dimension=1, tiled=True)]
    pallas_call x0 -> x4, Pallas kernels: none -> 239 us  [exchange(): pl.pallas_call(functools.partial(exchange_kernel, tuple(kinds), n_sum), o...]
    psum x3 -> x0, waiting for transfers between devices: 133 us -> none  [the longest x1 48.5 us: local(): lax.psum(jnp.dot(activated_b, w_down, preferred_element_type=jnp.float32)...]
    unnamed x1 -> x0, blocking collectives: 37.3 us -> none
    unnamed x73 -> x59, local copies, waits for them, and re-layouts: 10.4 us -> 4.61 us
  transfers between devices with their start and end apart: 7 -> 0, of which waited for: 7 -> 0; matrix products, arithmetic and copies ran while one was open for 6% -> 0% of each run, Pallas kernels for 0% -> 0%
where the time goes in v1:
time: 298 us; the launch traced here: 297 us
  Pallas kernels  239 us (80%)
  matrix products  31.1 us (10%)
  other arithmetic  17.2 us (6%)
  local copies, waits for them, and re-layouts  9.42 us (3%)
    pallas_call x4, Pallas kernels, exchange(): pl.pallas_call(functools.partial(exchange_kernel, tuple(kinds), n_sum), o...  239 us

profile of v1, /device:TPU:0, one launch (start us, length us, event | category | flops | bytes accessed | tf_op | source)
XLA Modules:
  0.0 297.5 jit_solution(15501588442752993829)
XLA Ops:
  1.6 1.3 convert_reduce_fusion
  2.9 1.5 fusion.14
  5.2 3.1 %fusion.22 = bf16[384,768]{1,0:T(8,128)(2,1)} fusion(bf16[1024,768]{1,0:T(8,128)(2,1)} %param.20, f32[768]{0:T(1024)S(1)} %copy-done.22, bf16[384,1024]{1,0:T(8,128)(2,1)S(1)} %copy-done.1, f32[1024]{0:T(1024)S(1)} %copy-done.19, f32[1024]{0:T(1024)S(1)} %copy-done.17, f32[384]{0:T(512)S(1)} %add_rsqrt_fusion.1, f32[384]{0:T(512)S(1)} %broadcast_multiply_fusion.5), kind=kOutput, calls=%fused_computation.45 | convolution fusion | flops 606928896 | bytes 2963456 | tf_op jit(solution)/shard_map/dot_general | solution.py:359
  8.3 1.4 copy.46
  9.8 1.7 fusion.46
  12.9 1.5 fusion.48.refs_0_
  14.4 26.0 %shard_map.254 = f32[384,1024]{1,0:T(8,128)} custom-call(f32[384,1024]{1,0:T(8,128)} %fusion.48.refs_0_), custom_call_target="tpu_custom_call" | custom-call | tf_op jit(solution)/shard_map/pallas_call | solution.py:284
  40.5 1.8 fusion.44
  44.3 1.8 fusion.47
  46.1 2.2 fusion.31.refs_2_
  48.2 2.4 fusion.41.refs_3_
  50.6 3.4 %fusion.42.refs_1_ = f32[1024,1024]{1,0:T(8,128)} fusion(bf16[384,1024]{1,0:T(8,128)(2,1)S(1)} %copy-done.5, f32[384,1024]{1,0:T(8,128)S(1)} %convolution_add_fusion), kind=kOutput, calls=%fused_computation.99 | convolution fusion | flops 808845312 | bytes 6553600 | tf_op jit(solution)/shard_map/dot_general | solution.py:385
  54.0 3.4 %fusion.33.refs_0_ = f32[1024,1024]{1,0:T(8,128)} fusion(bf16[384,1024]{1,0:T(8,128)(2,1)S(1)} %get-tuple-element.54, f32[384,1024]{1,0:T(8,128)S(1)} %get-tuple-element.39, f32[1024]{0:T(1024)S(1)} %copy-done.16, f32[1024]{0:T(1024)S(1)} %copy-done.14, f32[384]{0:T(512)S(1)} %add_rsqrt_fusion, f32[384]{0:T(512)S(1)} %broadcast_multiply_fusion.4), kind=kOutput, calls=%fused_computation.64 | convolution fusion | flops 807272448 | bytes 6564864 | tf_op jit(solution)/shard_map/dot_general | solution.py:389
  57.3 126.7 %shard_map.255 = (f32[128,1024]{1,0:T(8,128)}, f32[1024,128]{1,0:T(8,128)}, f32[384,1024]{1,0:T(8,128)}, f32[384,1024]{1,0:T(8,128)}) custom-call(f32[1024,1024]{1,0:T(8,128)} %fusion.33.refs_0_, f32[1024,1024]{1,0:T(8,128)} %fusion.42.refs_1_, f32[384,1024]{1,0:T(8,128)} %fusion.31.refs_2_, f32[384,1024]{1,0:T(8,128)} %fusion.41.refs_3_), custom_call_target="tpu_custom_call" | custom-call | tf_op jit(solution)/shard_map/pallas_call | solution.py:284
  184.1 2.2 multiply_reduce_fusion.1
  186.4 1.7 fusion.43
  189.6 1.4 fusion.28.refs_1_
  193.4 3.4 %fusion.49.refs_2_ = f32[384,1024]{1,0:T(8,128)} fusion(bf16[384,768]{0,1:T(8,128)(2,1)S(1)} %bitcast.97, bf16[1024,768]{1,0:T(8,128)(2,1)} %param.20), kind=kOutput, calls=%fused_computation.105 | convolution fusion | flops 603979776 | bytes 3735552 | tf_op jit(solution)/shard_map/dot_general | solution.py:431
  196.8 2.9 fusion.38.refs_0_
  199.6 70.4 %shard_map.256 = (f32[128,768]{1,0:T(8,128)}, f32[256,128]{1,0:T(8,128)}, f32[384,1024]{1,0:T(8,128)}) custom-call(f32[1024,768]{1,0:T(8,128)} %fusion.38.refs_0_, f32[256,1024]{1,0:T(8,128)} %fusion.28.refs_1_, f32[384,1024]{1,0:T(8,128)} %fusion.49.refs_2_), custom_call_target="tpu_custom_call" | custom-call | tf_op jit(solution)/shard_map/pallas_call | solution.py:284
  270.1 2.2 fusion.13
  272.4 3.2 %fusion.12 = f32[384,1024]{1,0:T(8,128)} fusion(f32[384,1024]{1,0:T(8,128)S(1)} %copy-done.3, bf16[384,1024]{1,0:T(8,128)(2,1)S(1)} %copy-done.1, f32[384,1024]{1,0:T(8,128)} %get-tuple-element.23, f32[384]{0:T(512)S(1)} %broadcast_multiply_fusion, f32[384]{0:T(512)S(1)} %broadcast_multiply_fusion.1, f32[1024]{0:T(1024)S(1)} %copy-done.17, ...), kind=kLoop, calls=%fused_computation.24 | loop fusion | flops 3538944 | bytes 5515264 | tf_op jit(solution)/shard_map/add | solution.py:437
  276.2 15.6 %shard_map.257 = f32[8,128]{1,0:T(8,128)} custom-call(f32[64,128]{1,0:T(8,128)} %bitcast.108), custom_call_target="tpu_custom_call" | custom-call | tf_op jit(solution)/shard_map/pallas_call | solution.py:284
  293.0 1.5 slice_bitcast_fusion.9
  (89 shorter events, 13.7 us)
Async XLA Ops:
  0.6 43.5 %copy-start = (bf16[1024,1024]{1,0:T(8,128)(2,1)S(1)}, bf16[1024,1024]{1,0:T(8,128)(2,1)}, u32[]{:S(2)}) copy-start(bf16[1024,1024]{1,0:T(8,128)(2,1)} %param.28) | copy-start | bytes 6291460
  0.7 4.6 %copy-start.1 = (bf16[384,1024]{1,0:T(8,128)(2,1)S(1)}, bf16[384,1024]{1,0:T(8,128)(2,1)}, u32[]{:S(2)}) copy-start(bf16[384,1024]{1,0:T(8,128)(2,1)} %param.15) | copy-start | bytes 2359300
  0.7 4.5 %copy-start.17 = (f32[1024]{0:T(1024)S(1)}, f32[1024]{0:T(1024)}, u32[]{:S(2)}) copy-start(f32[1024]{0:T(1024)} %param.18) | copy-start | bytes 12292
  0.7 4.5 %copy-start.19 = (f32[1024]{0:T(1024)S(1)}, f32[1024]{0:T(1024)}, u32[]{:S(2)}) copy-start(f32[1024]{0:T(1024)} %param.19) | copy-start | bytes 12292
  0.7 4.5 %copy-start.22 = (f32[768]{0:T(1024)S(1)}, f32[768]{0:T(1024)}, u32[]{:S(2)}) copy-start(f32[768]{0:T(1024)} %param.21) | copy-start | bytes 9220
  11.9 1.0 copy-start.6
  12.4 2.1 copy-start.8
  14.4 26.1 %copy-start.20 = (f32[1024]{0:T(1024)S(1)}, f32[1024]{0:T(1024)}, u32[]{:S(2)}) copy-start(f32[1024]{0:T(1024)} %param.23) | copy-start | bytes 12292
  40.5 2.2 copy-start.21
  42.4 0.7 copy-start.14
  42.4 0.8 copy-start.16
  42.4 0.8 copy-start.23
  43.1 1.1 copy-start.5
  184.1 2.3 copy-start.4
  184.1 2.3 copy-start.10
  184.1 2.3 copy-start.18
  186.4 1.7 copy-start.7
  188.1 1.1 copy-start.2
  188.6 1.0 copy-start.9
  270.1 2.3 copy-start.3
  272.4 22.1 %copy-start.13 = (f32[128,768]{1,0:T(8,128)S(1)}, f32[128,768]{1,0:T(8,128)}, u32[]{:S(2)}) copy-start(f32[128,768]{1,0:T(8,128)} %get-tuple-element.77) | copy-start | bytes 1179652
  272.4 22.9 %copy-start.15 = (f32[256,128]{1,0:T(8,128)S(1)}, f32[256,128]{1,0:T(8,128)}, u32[]{:S(2)}) copy-start(f32[256,128]{1,0:T(8,128)} %get-tuple-element.79) | copy-start | bytes 393220
  275.5 20.4 %copy-start.12 = (f32[128,1024]{1,0:T(8,128)S(1)}, f32[128,1024]{1,0:T(8,128)}, u32[]{:S(2)}) copy-start(f32[128,1024]{1,0:T(8,128)} %get-tuple-element.83) | copy-start | bytes 1572868
  275.5 21.2 %copy-start.11 = (f32[1024,128]{1,0:T(8,128)S(1)}, f32[1024,128]{1,0:T(8,128)}, u32[]{:S(2)}) copy-start(f32[1024,128]{1,0:T(8,128)} %get-tuple-element.85) | copy-start | bytes 1572868

commit v2 on v1

--- a/solution.py
+++ b/solution.py
@@ -50,6 +50,7 @@
     )
 
 CHUNKS = 4
+PIECES = 2
 LAG = 2
 MESH = pl.DeviceIdType.MESH
 MIB = 1024 * 1024
@@ -70,7 +71,7 @@
     lax.fori_loop(0, rows // step, body, 0)
 
 
-def exchange_kernel(kinds, n_sum, *refs):
+def exchange_kernel(kinds, n_sum, n_late, n_extra, middle, *refs):
     n_red = len(kinds)
     refs = list(refs)
 
@@ -79,14 +80,20 @@
         del refs[:count]
         return taken
 
-    grads, parts = take(n_red), take(n_sum)
+    late_sum = 1 if middle else 0
+    grads, parts = take(n_red - n_late), take(n_sum - late_sum)
+    extra = take(n_extra)
     outs, sums = take(n_red), take(n_sum)
+    more = take(2) if middle else []
     rx, ru, rd = take(n_red), take(n_red), take(n_red)
     if n_red:
         xs, xr, us, ur, ds, dr = take(6)
     if n_sum:
         near, mine, far = take(3)
         cs, cr, ys, yr, bs, br = take(6)
+    if middle:
+        grads += take(n_late)
+        parts += take(1)
     barrier = pltpu.get_barrier_semaphore()
     expected = 0
     if n_red:
@@ -116,14 +123,25 @@
         expected = expected + 2
     pl.semaphore_wait(barrier, expected)
 
-    def shard(m, target, column):
+    def shard(m, target, column, p):
         ref = grads[m]
         index = 2 * target + column
         if kinds[m] == "rows":
             size = ref.shape[0] // 8
-            return ref.at[pl.ds(pl.multiple_of(index * size, size), size), :]
+            piece = size // pieces(m)
+            start = pl.multiple_of(index * size + p * piece, piece)
+            return ref.at[pl.ds(start, piece), :]
         size = ref.shape[1] // 8
-        return ref.at[:, pl.ds(pl.multiple_of(index * size, size), size)]
+        piece = ref.shape[0] // pieces(m)
+        start = pl.multiple_of(index * size, size)
+        return ref.at[pl.ds(p * piece, piece), pl.ds(start, size)]
+
+    def pieces(m):
+        return PIECES if outs[m].shape[0] % (8 * PIECES) == 0 else 1
+
+    def slot(ref, m, t, p):
+        piece = outs[m].shape[0] // pieces(m)
+        return ref[m].at[t, pl.ds(p * piece, piece), :]
 
     def send(src, dst, send_sem, recv_sem, device):
         return pltpu.make_async_remote_copy(
@@ -135,14 +153,19 @@
             device_id_type=MESH,
         )
 
-    def across(m, t):
-        return send(shard(m, t, 1 - x), rx[m].at[t], xs.at[m, t], xr.at[m, t], other_x)
-
-    def up(m, t):
-        return send(rx[m].at[t], ru[m].at[t], us.at[m, t], ur.at[m, t], above)
-
-    def down(m, t):
-        return send(rx[m].at[t], rd[m].at[t], ds.at[m, t], dr.at[m, t], below)
+    def across(m, t, p):
+        return send(
+            shard(m, t, 1 - x, p), slot(rx, m, t, p), xs.at[m, t, p], xr.at[m, t, p], other_x
+        )
+
+    def up(m, t, p):
+        return send(
+            slot(rx, m, t, p), slot(ru, m, t, p), us.at[m, t, p], ur.at[m, t, p], above
+        )
+
+    def down(m, t, p, last=False):
+        dst = slot(rd, m, 0, p) if last else slot(ru, m, t, p)
+        return send(slot(rx, m, t, p), dst, ds.at[m, t, p], dr.at[m, t, p], below)
 
     def near_copy(a, k):
         half = parts[a].shape[0] // 2
@@ -170,12 +193,22 @@
             sums[a].at[rows, :], sums[a].at[rows, :], bs.at[a, k], br.at[a, k], other_core
         )
 
-    for a in range(n_sum):
+    def pieces_of(ms):
+        return [(m, t, p) for m in ms for t in (3, 0, 2, 1) for p in range(pieces(m))]
+
+    def start_sum(a):
         for k in range(CHUNKS):
             near_copy(a, k).start()
-    order = [(m, t) for m in range(n_red) for t in (3, 0, 2, 1)]
-    for m, t in order:
-        across(m, t).start()
+
+    def start_across(m):
+        for piece in pieces_of([m]):
+            across(*piece).start()
+
+    for a in range(n_sum - late_sum):
+        start_sum(a)
+    for m in range(n_red - n_late):
+        start_across(m)
+    order = pieces_of(range(n_red))
 
     def open_sum(a, k):
         near_copy(a, k).wait_recv()
@@ -187,110 +220,289 @@
         add_rows(sums[a].at[own(a, k), :], [mine.at[a, k], far.at[a, k]])
         back_copy(a, k).start()
 
-    def first_hop(m, t):
-        across(m, t).wait_recv()
-        add_rows(rx[m].at[t], [shard(m, t, x), rx[m].at[t]])
+    def first_hop(m, t, p):
+        across(m, t, p).wait_recv()
+        add_rows(slot(rx, m, t, p), [shard(m, t, x, p), slot(rx, m, t, p)])
         if t > 0:
 
             @pl.when(z == 0)
             def _():
-                up(m, t).start()
+                up(m, t, p).start()
 
         if t < 3:
 
             @pl.when(z == 3)
             def _():
-                down(m, t).start()
-
-    def next_hop(m, t):
+                down(m, t, p, t == 2).start()
+
+    def next_hop(m, t, p):
         @pl.when((z > 0) & (z < t))
         def _():
-            up(m, t).wait_recv()
-            add_rows(rx[m].at[t], [rx[m].at[t], ru[m].at[t]])
-            up(m, t).start()
-
-        @pl.when((z < 3) & (z > t))
-        def _():
-            down(m, t).wait_recv()
-            add_rows(rx[m].at[t], [rx[m].at[t], rd[m].at[t]])
-            down(m, t).start()
-
-    def last_hop(m, t):
+            up(m, t, p).wait_recv()
+            add_rows(slot(rx, m, t, p), [slot(rx, m, t, p), slot(ru, m, t, p)])
+            up(m, t, p).start()
+
+        for here in (1, 2):
+            if here > t:
+
+                @pl.when(z == here)
+                def _():
+                    down(m, t, p).wait_recv()
+                    add_rows(slot(rx, m, t, p), [slot(rx, m, t, p), slot(ru, m, t, p)])
+                    down(m, t, p, t == here - 1).start()
+
+    def last_hop(m, t, p):
         @pl.when(z == t)
         def _():
-            terms = [rx[m].at[t]]
+            terms = [slot(rx, m, t, p)]
             if t > 0:
-                up(m, t).wait_recv()
-                terms.append(ru[m].at[t])
+                up(m, t, p).wait_recv()
+                terms.append(slot(ru, m, t, p))
             if t < 3:
-                down(m, t).wait_recv()
-                terms.append(rd[m].at[t])
-            add_rows(outs[m], terms)
-
+                down(m, t, p).wait_recv()
+                terms.append(slot(rd, m, 0, p))
+            piece = outs[m].shape[0] // pieces(m)
+            add_rows(outs[m].at[pl.ds(p * piece, piece), :], terms)
+
+    state = {"first": 0, "next": 0}
+
+    def hop():
+        n = state["first"]
+        if n < len(order):
+            first_hop(*order[n])
+            state["first"] += 1
+        if state["next"] < len(order) and n >= state["next"] + LAG:
+            next_hop(*order[state["next"]])
+            state["next"] += 1
+
+    early = range(n_sum - late_sum)
+    for a in early:
+        for k in range(CHUNKS):
+            open_sum(a, k)
+    if middle:
+        hop()
+        hop()
+    for k in range(CHUNKS):
+        if n_sum:
+            close_sum(0, k)
+    if middle:
+        for k in range(CHUNKS):
+            back_copy(0, k).wait_recv()
+        steps = middle(sums[0], extra, more, grads[n_red - n_late :], parts[-1], refs)
+        closing = [(a, k) for a in early if a for k in range(CHUNKS)]
+        for step, started in steps:
+            step()
+            if started is not None:
+                start_across(n_red - n_late + started)
+            if closing:
+                close_sum(*closing.pop(0))
+            hop()
+        while closing:
+            close_sum(*closing.pop(0))
+        start_sum(n_sum - 1)
+        hop()
+        for k in range(CHUNKS):
+            open_sum(n_sum - 1, k)
+        hop()
+        hop()
+        hop()
+        for k in range(CHUNKS):
+            close_sum(n_sum - 1, k)
+    else:
+        for a in early:
+            for k in range(CHUNKS):
+                if a:
+                    close_sum(a, k)
+    while state["next"] < len(order) if n_red else False:
+        hop() if state["first"] < len(order) else drain(state, next_hop, order)
+    for piece in order:
+        last_hop(*piece)
     for a in range(n_sum):
         for k in range(CHUNKS):
-            open_sum(a, k)
-    closing = [(a, k) for a in range(n_sum) for k in range(CHUNKS)]
-    for n in range(len(order) + LAG):
-        if n > 0 or not order:
-            for _ in range(CHUNKS):
-                if closing:
-                    close_sum(*closing.pop(0))
-        if n < len(order):
-            first_hop(*order[n])
-        if n >= LAG and order:
-            next_hop(*order[n - LAG])
-    while closing:
-        close_sum(*closing.pop(0))
-    for m, t in order:
-        last_hop(m, t)
-    for a in range(n_sum):
-        for k in range(CHUNKS):
-            back_copy(a, k).wait_recv()
+            if not (middle and a == 0):
+                back_copy(a, k).wait_recv()
             near_copy(a, k).wait_send()
             far_copy(a, k).wait_send()
             back_copy(a, k).wait_send()
-    for m, t in order:
-        across(m, t).wait_send()
+    for m, t, p in order:
+        across(m, t, p).wait_send()
 
         @pl.when(z < t)
         def _():
-            up(m, t).wait_send()
+            up(m, t, p).wait_send()
 
         @pl.when(z > t)
         def _():
-            down(m, t).wait_send()
-
-
-def exchange(grads, kinds, parts, collective_id):
-    n_red, n_sum = len(grads), len(parts)
+            down(m, t, p).wait_send()
+
+
+def drain(state, next_hop, order):
+    next_hop(*order[state["next"]])
+    state["next"] += 1
+
+
+def contract(left, right, left_axis, right_axis):
+    return lax.dot_general(
+        left, right, (((left_axis,), (right_axis,)), ((), ())), preferred_element_type=jnp.float32
+    )
+
+
+def backward_steps(grad_norm2, extra, more, grads, part, scratch):
+    (
+        cotangent,
+        normed2,
+        inverse2,
+        gain2,
+        context_t,
+        w_dense_t,
+        probs,
+        queries,
+        key_vecs,
+        val_vecs,
+        first_in_t,
+        w_qkv_t,
+    ) = extra
+    grad_hidden, grad_joined = more
+    grad_w_dense, grad_w_qkv = grads
+    grad_hidden_b, grad_context, thirds, grad_joined_b = scratch
+    heads = probs.shape[0]
+    rows = cotangent.shape[0]
+    scaling = 1.0 / math.sqrt(HD)
+
+    def hidden_step():
+        def body(i, carry):
+            at = pl.ds(pl.multiple_of(i * 16, 16), 16)
+            change = norm_backward(
+                grad_norm2[at, :], normed2[at, :], inverse2[at, :], gain2[...]
+            )
+            value = cotangent[at, :].astype(jnp.float32) + change
+            grad_hidden[at, :] = value
+            grad_hidden_b[at, :] = value.astype(jnp.bfloat16)
+            return carry
+
+        lax.fori_loop(0, rows // 16, body, 0)
+
+    def dense_step():
+        def body(i, carry):
+            at = pl.ds(pl.multiple_of(i * 64, 64), 64)
+            grad_w_dense[at, :] = contract(context_t[at, :], grad_hidden_b[...], 1, 0)
+            return carry
+
+        lax.fori_loop(0, context_t.shape[0] // 64, body, 0)
+
+    def context_step():
+        def body(i, carry):
+            at = pl.ds(pl.multiple_of(i * 128, 128), 128)
+            value = contract(grad_hidden_b[at, :], w_dense_t[...], 1, 0).astype(jnp.bfloat16)
+            for h in range(heads):
+                grad_context[h, at, :] = value[:, h * HD : (h + 1) * HD]
+            return carry
+
+        lax.fori_loop(0, rows // 128, body, 0)
+
+    def attention_step():
+        def body(h, carry):
+            prob = probs[h]
+            upstream = grad_context[h]
+            grad_probs = contract(upstream, val_vecs[h], 1, 1)
+            row_inner = jnp.sum(prob * grad_probs, axis=-1, keepdims=True)
+            grad_scores = (prob * (grad_probs - row_inner)).astype(jnp.bfloat16)
+            thirds[h, 2] = contract(prob.astype(jnp.bfloat16), upstream, 0, 0)
+            thirds[h, 0] = contract(grad_scores, key_vecs[h], 1, 0) * scaling
+            thirds[h, 1] = contract(grad_scores, queries[h], 0, 0) * scaling
+            return carry
+
+        lax.fori_loop(0, heads, body, 0)
+
+    def joined_step():
+        for h in range(heads):
+            for third in range(3):
+                start = (3 * h + third) * HD
+                grad_joined[:, start : start + HD] = thirds[h, third]
+
+        def body(i, carry):
+            at = pl.ds(pl.multiple_of(i * 32, 32), 32)
+            grad_joined_b[at, :] = grad_joined[at, :].astype(jnp.bfloat16)
+            return carry
+
+        lax.fori_loop(0, rows // 32, body, 0)
+
+    def qkv_step():
+        def body(i, carry):
+            at = pl.ds(pl.multiple_of(i * 128, 128), 128)
+            grad_w_qkv[at, :] = contract(first_in_t[at, :], grad_joined_b[...], 1, 0)
+            return carry
+
+        lax.fori_loop(0, first_in_t.shape[0] // 128, body, 0)
+
+    def norm_step():
+        def body(i, carry):
+            at = pl.ds(pl.multiple_of(i * 64, 64), 64)
+            part[at, :] = contract(grad_joined_b[at, :], w_qkv_t[...], 1, 0)
+            return carry
+
+        lax.fori_loop(0, rows // 64, body, 0)
+
+    return [
+        (hidden_step, None),
+        (dense_step, 0),
+        (context_step, None),
+        (attention_step, None),
+        (joined_step, None),
+        (qkv_step, 1),
+        (norm_step, None),
+    ]
+
+
+def exchange(grads, kinds, parts, collective_id, extra=(), middle=None):
     f32 = jnp.float32
-    shapes = []
-    for grad, kind in zip(grads, kinds):
-        rows, columns = grad.shape
+    shapes, full, late = [], [g.shape for g in grads], []
+    sums = [p.shape for p in parts]
+    more = []
+    kinds = list(kinds)
+    if middle:
+        rows, width = extra[0].shape
+        columns = extra[4].shape[0]
+        late = [(columns, width), (width, 3 * columns)]
+        kinds += ["columns", "rows"]
+        sums.append((rows, width))
+        more = [(rows, width), (rows, 3 * columns)]
+    for (rows, columns), kind in zip(full + late, kinds):
         shapes.append((rows // 8, columns) if kind == "rows" else (rows, columns // 8))
-    out_shape = [jax.ShapeDtypeStruct(s, f32) for s in shapes]
-    out_shape += [jax.ShapeDtypeStruct(p.shape, f32) for p in parts]
+    n_red, n_sum = len(shapes), len(sums)
+    out_shape = [jax.ShapeDtypeStruct(s, f32) for s in shapes + sums + more]
     scratch = []
     if n_red:
-        for _ in range(3):
-            scratch += [pltpu.VMEM((4,) + s, f32) for s in shapes]
-        scratch += [pltpu.SemaphoreType.DMA((n_red, 4))] * 6
+        for slots in (4, 4, 1):
+            scratch += [pltpu.VMEM((slots,) + s, f32) for s in shapes]
+        scratch += [pltpu.SemaphoreType.DMA((n_red, 4, PIECES))] * 6
     if n_sum:
-        rows, columns = parts[0].shape
+        rows, columns = sums[0]
         scratch += [pltpu.VMEM((n_sum, CHUNKS, rows // 2 // CHUNKS, columns), f32)] * 3
         scratch += [pltpu.SemaphoreType.DMA((n_sum, CHUNKS))] * 6
+    if middle:
+        heads, rows, _ = extra[6].shape
+        width = extra[0].shape[1]
+        scratch += [pltpu.VMEM(s, f32) for s in late] + [pltpu.VMEM(sums[-1], f32)]
+        scratch += [
+            pltpu.VMEM((rows, width), jnp.bfloat16),
+            pltpu.VMEM((heads, rows, HD), jnp.bfloat16),
+            pltpu.VMEM((heads, 3, rows, HD), f32),
+            pltpu.VMEM((rows, 3 * heads * HD), jnp.bfloat16),
+        ]
     vmem = pl.BlockSpec(memory_space=pltpu.VMEM)
     return pl.pallas_call(
-        functools.partial(exchange_kernel, tuple(kinds), n_sum),
+        functools.partial(exchange_kernel, tuple(kinds), n_sum, len(late), len(extra), middle),
         out_shape=out_shape,
-        in_specs=[vmem] * (n_red + n_sum),
-        out_specs=[vmem] * (n_red + n_sum),
+        in_specs=[vmem] * (len(grads) + len(parts) + len(extra)),
+        out_specs=[vmem] * len(out_shape),
         scratch_shapes=scratch,
         compiler_params=pltpu.CompilerParams(
-            collective_id=collective_id, has_side_effects=True, vmem_limit_bytes=56 * MIB
+            collective_id=collective_id,
+            has_side_effects=True,
+            vmem_limit_bytes=(63 if middle else 40) * MIB,
         ),
-    )(*grads, *parts)
+    )(*grads, *parts, *extra)
 
 
 def paired(size_tensor):
@@ -366,7 +578,8 @@
     scores = head_scores(queries, key_vecs, slopes, offset, allowed, scaling)
     highest = jnp.max(scores, axis=-1, keepdims=True)
     log_total = highest + jnp.log(jnp.sum(jnp.exp(scores - highest), axis=-1, keepdims=True))
-    probs_b = jnp.exp(scores - log_total).astype(jnp.bfloat16)
+    probs = jnp.exp(scores - log_total)
+    probs_b = probs.astype(jnp.bfloat16)
     context = jnp.einsum(
         "hij,jhe->ihe", probs_b, val_vecs, preferred_element_type=jnp.float32
     ).astype(jnp.bfloat16)
@@ -389,49 +602,83 @@
     grad_w_up = jnp.dot(second_in.T, grad_up_b, preferred_element_type=jnp.float32)
     grad_b_up = jnp.sum(grad_up, axis=0)
     grad_norm2 = jnp.dot(grad_up_b, w_up.T, preferred_element_type=jnp.float32)
-    (grad_w_up, grad_w_down), (grad_norm2, mixed) = scatter(
-        [grad_w_up, grad_w_down], ["rows", "columns"], [grad_norm2, mixed], sizes, 1
-    )
+    if sizes == (8, 4):
+        extra = (
+            cotangent,
+            normed2,
+            inverse2,
+            norm2_gain[None],
+            context.T,
+            w_dense.T,
+            probs,
+            queries.transpose(1, 0, 2),
+            key_vecs.transpose(1, 0, 2),
+            val_vecs.transpose(1, 0, 2),
+            first_in.T,
+            w_qkv.T,
+        )
+        (
+            grad_w_up,
+            grad_w_down,
+            grad_w_dense,
+            grad_w_qkv,
+            grad_norm2,
+            mixed,
+            grad_norm1,
+            grad_hidden,
+            grad_joined,
+        ) = exchange(
+            [grad_w_up, grad_w_down],
+            ["rows", "columns"],
+            [grad_norm2, mixed],
+            1,
+            extra,
+            backward_steps,
+        )
+    else:
+        (grad_w_up, grad_w_down), (grad_norm2, mixed) = scatter(
+            [grad_w_up, grad_w_down], ["rows", "columns"], [grad_norm2, mixed], sizes, 1
+        )
+        grad_hidden = grad_out + norm_backward(grad_norm2, normed2, inverse2, norm2_gain)
+        grad_hidden_b = grad_hidden.astype(jnp.bfloat16)
+        grad_w_dense = jnp.dot(context.T, grad_hidden_b, preferred_element_type=jnp.float32)
+        grad_context = jnp.dot(grad_hidden_b, w_dense.T, preferred_element_type=jnp.float32).astype(
+            jnp.bfloat16
+        )
+        grad_context = grad_context.reshape(row_count, heads_here, HD)
+        scores_again = head_scores(queries, key_vecs, slopes, offset, allowed, scaling)
+        probs_again = jnp.exp(scores_again - log_total)
+        probs_again_b = probs_again.astype(jnp.bfloat16)
+        grad_vals = jnp.einsum(
+            "hij,ihe->jhe", probs_again_b, grad_context, preferred_element_type=jnp.float32
+        )
+        grad_probs = jnp.einsum(
+            "ihe,jhe->hij", grad_context, val_vecs, preferred_element_type=jnp.float32
+        )
+        row_inner = jnp.sum(probs_again * grad_probs, axis=-1, keepdims=True)
+        grad_scores = (probs_again * (grad_probs - row_inner)).astype(jnp.bfloat16)
+        grad_queries = (
+            jnp.einsum("hij,jhe->ihe", grad_scores, key_vecs, preferred_element_type=jnp.float32)
+            * scaling
+        )
+        grad_keys = (
+            jnp.einsum("hij,ihe->jhe", grad_scores, queries, preferred_element_type=jnp.float32)
+            * scaling
+        )
+        grad_joined = jnp.stack([grad_queries, grad_keys, grad_vals], axis=2).reshape(
+            row_count, 3 * heads_here * HD
+        )
+        grad_joined_b = grad_joined.astype(jnp.bfloat16)
+        grad_w_qkv = jnp.dot(first_in.T, grad_joined_b, preferred_element_type=jnp.float32)
+        grad_norm1 = jnp.dot(grad_joined_b, w_qkv.T, preferred_element_type=jnp.float32)
+        (grad_w_qkv, grad_w_dense), (grad_norm1,) = scatter(
+            [grad_w_qkv, grad_w_dense], ["rows", "columns"], [grad_norm1], sizes, 2
+        )
     output = (hidden + mixed + b_down).astype(jnp.bfloat16)
     grad_gain2 = jnp.sum(grad_norm2 * normed2, axis=0)
     grad_shift2 = jnp.sum(grad_norm2, axis=0)
-    grad_hidden = grad_out + norm_backward(grad_norm2, normed2, inverse2, norm2_gain)
-    grad_hidden_b = grad_hidden.astype(jnp.bfloat16)
-    grad_w_dense = jnp.dot(context.T, grad_hidden_b, preferred_element_type=jnp.float32)
     grad_b_dense = jnp.sum(grad_hidden, axis=0)
-    grad_context = jnp.dot(grad_hidden_b, w_dense.T, preferred_element_type=jnp.float32).astype(
-        jnp.bfloat16
-    )
-    grad_context = grad_context.reshape(row_count, heads_here, HD)
-    scores_again = head_scores(queries, key_vecs, slopes, offset, allowed, scaling)
-    probs_again = jnp.exp(scores_again - log_total)
-    probs_again_b = probs_again.astype(jnp.bfloat16)
-    grad_vals = jnp.einsum(
-        "hij,ihe->jhe", probs_again_b, grad_context, preferred_element_type=jnp.float32
-    )
-    grad_probs = jnp.einsum(
-        "ihe,jhe->hij", grad_context, val_vecs, preferred_element_type=jnp.float32
-    )
-    row_inner = jnp.sum(probs_again * grad_probs, axis=-1, keepdims=True)
-    grad_scores = (probs_again * (grad_probs - row_inner)).astype(jnp.bfloat16)
-    grad_queries = (
-        jnp.einsum("hij,jhe->ihe", grad_scores, key_vecs, preferred_element_type=jnp.float32)
-        * scaling
-    )
-    grad_keys = (
-        jnp.einsum("hij,ihe->jhe", grad_scores, queries, preferred_element_type=jnp.float32)
-        * scaling
-    )
-    grad_joined = jnp.stack([grad_queries, grad_keys, grad_vals], axis=2).reshape(
-        row_count, 3 * heads_here * HD
-    )
-    grad_joined_b = grad_joined.astype(jnp.bfloat16)
-    grad_w_qkv = jnp.dot(first_in.T, grad_joined_b, preferred_element_type=jnp.float32)
     grad_b_qkv = jnp.sum(grad_joined, axis=0)
-    grad_norm1 = jnp.dot(grad_joined_b, w_qkv.T, preferred_element_type=jnp.float32)
-    (grad_w_qkv, grad_w_dense), (grad_norm1,) = scatter(
-        [grad_w_qkv, grad_w_dense], ["rows", "columns"], [grad_norm1], sizes, 2
-    )
     grad_gain1 = jnp.sum(grad_norm1 * normed1, axis=0)
     grad_shift1 = jnp.sum(grad_norm1, axis=0)
     grad_input = grad_hidden + norm_backward(grad_norm1, normed1, inverse1, norm1_gain)

time: 298 us -> 276 us (0.926)
  Pallas kernels: 239 us -> 202 us
  local copies, waits for them, and re-layouts: 9.42 us -> 37.5 us
  matrix products: 31.1 us -> 17.5 us
    pallas_call x4 -> x3, Pallas kernels: 239 us -> 202 us  [exchange(): pl.pallas_call(functools.partial(exchange_kernel, tuple(kinds), n_sum, le...]
    unnamed x59 -> x84, local copies, waits for them, and re-layouts: 4.61 us -> 20.7 us
    pallas_call x0 -> x5, local copies, waits for them, and re-layouts: none -> 11.4 us  [exchange(): pl.pallas_call(functools.partial(exchange_kernel, tuple(kinds), n_sum, le...]
    dot_general x8 -> x0, matrix products: 10.1 us -> none  [the longest x1 3.37 us: local(): jnp.dot(grad_joined_b, w_qkv.T, preferred_element_type=jnp.float32)]
    reduce_sum x0 -> x3, other arithmetic: none -> 3.44 us  [the longest x1 1.66 us: local(): grad_shift2 = jnp.sum(grad_norm2, axis=0)]
where the time goes in v2:
time: 276 us; the launch traced here: 275 us
  Pallas kernels  202 us (73%)
  local copies, waits for them, and re-layouts  37.5 us (14%)
  matrix products  17.5 us (6%)
  other arithmetic  16.9 us (6%)
    pallas_call x3, Pallas kernels, exchange(): pl.pallas_call(functools.partial(exchange_kernel, tuple(kinds), n_sum, le...  202 us
    unnamed x84, local copies, waits for them, and re-layouts  20.7 us
    pallas_call x5, local copies, waits for them, and re-layouts, exchange(): pl.pallas_call(functools.partial(exchange_kernel, tuple(kinds), n_sum, le...  11.4 us

profile of v2, /device:TPU:0, one launch (start us, length us, event | category | flops | bytes accessed | tf_op | source)
XLA Modules:
  0.0 275.1 jit_solution(10704554536489898491)
XLA Ops:
  8.7 23.5 %shard_map.254 = f32[384,1024]{1,0:T(8,128)S(1)} custom-call(f32[384,1024]{1,0:T(8,128)S(1)} %fusion.46.refs_0_), custom_call_target="tpu_custom_call" | custom-call | tf_op jit(solution)/shard_map/pallas_call | solution.py:494
  32.3 1.6 copy.54
  33.9 1.8 fusion.42
  40.3 2.4 fusion.45
  42.7 3.2 %fusion.30.refs_0_ = f32[1024,1024]{1,0:T(8,128)} fusion(bf16[384,1024]{1,0:T(8,128)(2,1)S(1)} %get-tuple-element.80, f32[384,1024]{0,1:T(8,128)S(1)} %get-tuple-element.66, f32[1024]{0:T(1024)S(1)} %copy-done.21, f32[1024]{0:T(1024)S(1)} %copy-done.20), kind=kOutput, calls=%fused_computation.48 | convolution fusion | flops 806486016 | bytes 6561792 | tf_op jit(solution)/shard_map/dot_general | solution.py:602
  45.9 3.4 %fusion.41.refs_1_ = f32[1024,1024]{1,0:T(8,128)} fusion(bf16[384,1024]{1,0:T(8,128)(2,1)S(1)} %copy-done.6, f32[384,1024]{1,0:T(8,128)S(1)} %convolution_add_fusion), kind=kOutput, calls=%fused_computation.74 | convolution fusion | flops 808845312 | bytes 6553600 | tf_op jit(solution)/shard_map/dot_general | solution.py:598
  49.3 2.2 fusion.28.refs_2_
  51.5 2.3 fusion.40.refs_3_
  53.8 1.7 copy.57.refs_5_
  57.0 1.8 copy.71
  58.9 1.8 copy.72
  60.7 1.9 copy.70
  62.6 1.6 copy.56
  65.2 156.3 %shard_map.255 = (f32[128,1024]{1,0:T(8,128)}, f32[1024,128]{1,0:T(8,128)}, f32[256,128]{1,0:T(8,128)}, f32[128,768]{1,0:T(8,128)}, f32[384,1024]{1,0:T(8,128)},...) custom-call(f32[1024,1024]{1,0:T(8,128)} %fusion.30.refs_0_, ...), custom_call_target="tpu_custom_call" | custom-call | tf_op jit(solution)/shard_map/pallas_call | solution.py:494
  221.5 3.2 %copy.63 = f32[384,1024]{0,1:T(8,128)} copy(f32[384,1024]{1,0:T(8,128)} %get-tuple-element.27) | data formatting | bytes 3145728 | tf_op jit(solution)/shard_map/pallas_call | solution.py:494
  224.7 2.2 multiply_reduce_fusion
  226.9 1.9 copy.60
  232.1 1.6 reduce_sum.143
  234.1 1.7 reduce_sum.147
  236.0 22.3 %shard_map.256 = f32[8,128]{1,0:T(8,128)S(1)} custom-call(f32[64,128]{1,0:T(8,128)S(1)} %bitcast.69), custom_call_target="tpu_custom_call" | custom-call | tf_op jit(solution)/shard_map/pallas_call | solution.py:494
  259.4 1.6 copy.59
  261.1 3.1 %copy.61 = f32[384,1024]{0,1:T(8,128)} copy(f32[384,1024]{1,0:T(8,128)} %get-tuple-element.24) | data formatting | bytes 3145728 | tf_op jit(solution)/shard_map/pallas_call | solution.py:494
  264.2 3.7 %fusion.11 = (f32[384,1024]{0,1:T(8,128)}, bf16[384,1024]{0,1:T(8,128)(2,1)S(1)}) fusion(f32[384,1024]{0,1:T(8,128)} %copy.61, bf16[384,1024]{0,1:T(8,128)(2,1)S(1)} %copy.45, f32[384,1024]{0,1:T(8,128)} %copy-done.5, f32[384]{0:T(512)S(1)} %get-tuple-element.81, f32[384]{0:T(512)S(1)} %get-tuple-element.82, f32[1024]{0:T(1024)S(1)} %copy-done.24, ...), kind=kLoop, calls=%fused_computation.19 | loop fusion | flops 5505024 | bytes 9455616 | tf_op jit(solution)/shard_map/add | solution.py:684
  267.9 3.0 %copy.65 = f32[384,1024]{1,0:T(8,128)} copy(f32[384,1024]{0,1:T(8,128)} %get-tuple-element.63) | data formatting | bytes 3145728
  (112 shorter events, 24.2 us)
Async XLA Ops:
  0.6 2.1 copy-start.24
  0.7 2.1 copy-start.31
  0.7 2.1 copy-start.12
  0.7 2.1 copy-start.35
  33.9 1.9 copy-start
  37.9 15.9 %copy-start.2 = (f32[384,1024]{0,1:T(8,128)}, f32[384,1024]{0,1:T(8,128)S(1)}, u32[]{:S(2)}) copy-start(f32[384,1024]{0,1:T(8,128)S(1)} %get-tuple-element.66) | copy-start | bytes 4718596
  38.0 2.3 copy-start.34
  55.4 7.2 %copy-start.13 = (bf16[1024,768]{1,0:T(8,128)(2,1)S(1)}, bf16[1024,768]{1,0:T(8,128)(2,1)}, u32[]{:S(2)}) copy-start(bf16[1024,768]{1,0:T(8,128)(2,1)} %param.20) | copy-start | bytes 4718596
  221.5 3.2 %copy-start.3 = (f32[384,1024]{0,1:T(8,128)S(1)}, f32[384,1024]{0,1:T(8,128)}, u32[]{:S(2)}) copy-start(f32[384,1024]{0,1:T(8,128)} %copy-done.2) | copy-start | bytes 4718596
  228.8 2.5 copy-start.5
  228.8 1.8 copy-start.15
  232.1 1.9 copy-start.8
  233.9 1.8 copy-start.7
  234.1 1.9 copy-start.25
  234.1 1.9 copy-start.26
  234.1 1.9 copy-start.30
  234.1 25.3 %copy-start.27 = (f32[384]{0:T(512)S(1)}, f32[384]{0:T(512)}, u32[]{:S(2)}) copy-start(f32[384]{0:T(512)} %get-tuple-element.61) | copy-start | bytes 4612
  234.1 25.3 %copy-start.28 = (f32[384]{0:T(512)S(1)}, f32[384]{0:T(512)}, u32[]{:S(2)}) copy-start(f32[384]{0:T(512)} %get-tuple-element.62) | copy-start | bytes 4612
  234.1 25.3 %copy-start.14 = (f32[384,1024]{1,0:T(8,128)S(1)}, f32[384,1024]{1,0:T(8,128)}, u32[]{:S(2)}) copy-start(f32[384,1024]{1,0:T(8,128)} %get-tuple-element.23) | copy-start | bytes 4718596
  261.1 3.1 %copy-start.1 = (f32[384,1024]{0,1:T(8,128)S(1)}, f32[384,1024]{0,1:T(8,128)}, u32[]{:S(2)}) copy-start(f32[384,1024]{0,1:T(8,128)} %copy.54) | copy-start | bytes 4718596
  261.1 3.1 %copy-start.29 = (f32[1024]{0:T(1024)S(1)}, f32[1024]{0:T(1024)}, u32[]{:S(2)}) copy-start(f32[1024]{0:T(1024)} %param.29) | copy-start | bytes 12292
  270.9 1.9 copy-start.19
  270.9 2.6 copy-start.17
  270.9 3.4 %copy-start.16 = (f32[1024,128]{1,0:T(8,128)S(1)}, f32[1024,128]{1,0:T(8,128)}, u32[]{:S(2)}) copy-start(f32[1024,128]{1,0:T(8,128)} %get-tuple-element.111) | copy-start | bytes 1572868
  (12 other events, 16.2 us)
